TPU v7x, 128 devices: a whole 4x4x4 slice. The times are simulated.
128 devices in a mesh: row: 8 (over x, z_hi), col: 16 (over z_lo, y, core).
Axes of the slice: x: 4, y: 4, z: 4 (z_hi: 2, z_lo: 2; z = z_hi * 2 + z_lo), core: 2. Of those that a mesh axis runs over, the one named last changes fastest.
Arguments:
- window: float32 [12288, 12288], P('row', 'col'), may hold values from -6 to 6
- reflectors: float32 [2, 12288, 256], P(None, 'row', 'col'), may hold values from -0.0546875 to 0.0546875
- factors: float32 [2, 256, 256], replicated, may hold values from -0.375 to 0.375
Outputs:
- updated: float32 [12288, 12288], P('row', 'col')
All inputs are finite; a program needn't handle non-finite values.
Results may differ from a plain program's by a relative error of at most 0.0001.
Values sent between devices are 32-bit elements; how exact they have to be, the bound alone decides.
A program may use at most 128 MiB of HBM per device.

v0:
```python
import jax
import jax.numpy as jnp
from jax import lax
from jax.sharding import PartitionSpec as P

HIGH = lax.Precision.HIGH


def mm(a, b, ca, cb):
    return lax.dot_general(
        a, b, (((ca,), (cb,)), ((), ())), precision=HIGH, preferred_element_type=jnp.float32
    )


def body(window, reflectors, factors):
    panels, rows, piece = reflectors.shape
    cols = window.shape[1]
    row_n = lax.axis_size("row")
    col_n = lax.axis_size("col")
    block = piece * col_n
    width = panels * block
    c = lax.axis_index("col")
    vt = jnp.swapaxes(reflectors, 1, 2)
    vr = lax.all_gather(vt, "col", axis=1, tiled=True).reshape(width, rows)
    halves = vt.reshape(panels, piece, 2, cols)
    k = c % 2
    own = lax.dynamic_index_in_dim(halves, k, 2, keepdims=False)
    other = lax.dynamic_index_in_dim(halves, 1 - k, 2, keepdims=False)
    pairs_a = []
    pairs_b = []
    for r in range(row_n):
        for cc in range(col_n):
            pairs_a.append((r * col_n + cc, cc // 2 * col_n + 2 * r + cc % 2))
            pairs_b.append((r * col_n + cc, cc // 2 * col_n + 2 * r + 1 - cc % 2))
    got_a = lax.ppermute(own, ("row", "col"), pairs_a)
    got_b = lax.ppermute(other, ("row", "col"), pairs_b)
    first = jnp.where(k == 0, got_a, got_b)
    second = jnp.where(k == 0, got_b, got_a)
    pair = jnp.stack([first, second], 1)
    vc = lax.all_gather(pair, "row", axis=1, tiled=True).reshape(width, cols)
    p_part = mm(vr, window, 1, 0)
    y_part = mm(window, vc, 1, 1)
    p_own = lax.psum_scatter(p_part, "row", scatter_dimension=0, tiled=True)
    y_own = lax.psum_scatter(y_part, "col", scatter_dimension=0, tiled=True)
    g12 = lax.psum(mm(vc[:block], vc[block:], 1, 1), "col")
    s_own = lax.psum(mm(p_own, vc, 1, 1), "col")
    t1, t2 = (factors[0], factors[1])
    t12 = -mm(mm(t1, g12, 1, 0), t2, 1, 0)
    tc = jnp.concatenate(
        [jnp.concatenate([t1, t12], 1), jnp.concatenate([jnp.zeros_like(t1), t2], 1)], 0
    )
    p_own = p_own - mm(mm(s_own, tc, 1, 0), vc, 1, 0)
    z_own = mm(y_own, tc, 1, 0)
    p_all = lax.all_gather(p_own, "row", axis=0, tiled=True)
    z_all = lax.all_gather(z_own, "col", axis=0, tiled=True)
    q = mm(tc, p_all, 0, 0)
    return window - mm(vr, q, 0, 0) - mm(z_all, vc, 1, 0)


def solution(mesh):
    placed = (P("row", "col"), P(None, "row", "col"), P())
    return jax.shard_map(
        body, mesh=mesh, in_specs=placed, out_specs=P("row", "col"), check_vma=False
    )
```

profile of v0, /device:TPU:1, one launch (start us, length us, event | category | flops | bytes accessed | tf_op | source)
XLA Modules:
  0.0 484.4 jit_solution(11163545829636249357)
XLA Ops:
  6.5 0.7 all-gather.7.cloned.1.call-update
  7.3 1.1 reshape.11
  8.4 0.2 constant_dynamic-slice_fusion.1
  8.6 1.5 collective-permute-start.1
  10.1 0.7 collective-permute-start
  10.7 0.3 collective-permute-done.1
  11.0 0.7 pad_maximum_fusion
  11.8 44.7 %all-gather.7.cloned.1.call-done = f32[2,256,1536]{2,1,0:T(8,128)} async-done(((f32[2,16,1536]{2,1,0:T(8,128)}), f32[2,256,1536]{2,1,0:T(8,128)}) %all-gather.7.cloned.1.call-update) | async-done | bytes 3145744 | tf_op jit(solution)/shard_map/all_gather | solution.py:24
  56.5 8.5 %fusion.21 = f32[512,768]{1,0:T(8,128)} fusion(f32[512,1536]{1,0:T(8,128)} %bitcast.55, f32[1536,768]{1,0:T(8,128)} %param.3), kind=kOutput, calls=%fused_computation.34 | convolution fusion | flops 3623878656 | bytes 9437184 | tf_op jit(solution)/shard_map/dot_general | solution.py:10
  65.1 42.1 %all-gather.5.cloned.1.call-done = f32[2,16,16,768]{3,2,1,0:T(8,128)} async-done(((f32[2,2,16,768]{3,2,1,0:T(8,128)}), f32[2,16,16,768]{3,2,1,0:T(8,128)}) %all-gather.5.cloned.1.call-update) | async-done | bytes 1572880 | tf_op jit(solution)/shard_map/all_gather | solution.py:40
  107.1 1.6 fusion.18
  108.7 1.2 fusion.20
  110.0 74.3 %reduce-scatter.5.cloned.1.call-done = f32[64,768]{1,0:T(8,128)} async-done(((f32[512,768]{1,0:T(8,128)}), f32[64,768]{1,0:T(8,128)}) %reduce-scatter.5.cloned.1.call-update) | async-done | bytes 196624 | tf_op jit(solution)/shard_map/reduce_scatter | solution.py:43
  184.3 2.4 fusion.22
  186.8 7.9 %convolution_bitcast_fusion = f32[1536,512]{0,1:T(8,128)} fusion(f32[512,768]{1,0:T(8,128)S(1)} %bitcast.52, f32[1536,768]{1,0:T(8,128)} %param.3), kind=kOutput, calls=%fused_computation.2 | convolution fusion | flops 3623878656 | bytes 9437184 | tf_op jit(solution)/shard_map/dot_general | solution.py:10
  194.7 3.6 copy.26
  198.3 0.2 all-gather.9.cloned.1.call-start
  198.5 0.8 copy-done.2
  199.6 106.0 %all-reduce.4.cloned.1.call-done = (f32[64,512]{1,0:T(8,128)}, f32[256,256]{1,0:T(8,128)}) async-done(((f32[64,512]{1,0:T(8,128)}, f32[256,256]{1,0:T(8,128)}), (f32[64,512]{1,0:T(8,128)}, f32[256,256]{1,0:T(8,128)})) %all-reduce.4.cloned.1.call-update) | async-done | bytes 393232 | tf_op jit(solution)/shard_map/psum | solution.py:46
  305.6 1.3 fusion.5
  307.0 0.4 convolution_negate_fusion
  307.4 1.4 fusion.3
  308.8 1.3 convolution_subtract_fusion
  310.1 60.9 %reduce-scatter.7.cloned.1.call-done = f32[96,512]{1,0:T(8,128)} async-done(((f32[1536,512]{1,0:T(8,128)}), f32[96,512]{1,0:T(8,128)}) %reduce-scatter.7.cloned.1.call-update) | async-done | bytes 196624
  371.0 2.1 fusion.1
  373.2 6.0 %copy.22 = f32[1536,768]{0,1:T(8,128)} copy(f32[1536,768]{1,0:T(8,128)} %param.3) | data formatting | bytes 9437184 | tf_op args[0]
  379.2 45.8 %all-gather.9.cloned.1.call-done = f32[512,768]{1,0:T(8,128)} async-done(((f32[64,768]{1,0:T(8,128)}), f32[512,768]{1,0:T(8,128)}) %all-gather.9.cloned.1.call-update) | async-done | bytes 1572880 | tf_op jit(solution)/shard_map/all_gather | solution.py:54
  425.0 3.0 fusion.2
  428.1 6.3 %fusion.23 = f32[768,1536]{1,0:T(8,128)} fusion(f32[512,768]{1,0:T(8,128)S(1)} %fusion.2, f32[512,1536]{1,0:T(8,128)S(1)} %bitcast.56), kind=kOutput, calls=%fused_computation.36 | convolution fusion | flops 3623878656 | bytes 9437184 | tf_op jit(solution)/shard_map/dot_general | solution.py:10
  434.3 28.2 %all-gather.11.cloned.1.call-done = f32[1536,512]{1,0:T(8,128)} async-done(((f32[96,512]{1,0:T(8,128)}), f32[1536,512]{1,0:T(8,128)}) %all-gather.11.cloned.1.call-update) | async-done | bytes 3145744 | tf_op jit(solution)/shard_map/all_gather | solution.py:55
  462.5 9.0 %fusion = f32[1536,768]{0,1:T(8,128)} fusion(f32[1536,768]{0,1:T(8,128)} %copy.22, f32[768,1536]{1,0:T(8,128)} %fusion.23, f32[1536,512]{1,0:T(8,128)} %all-gather.11.cloned.1.call-done, f32[512,768]{1,0:T(8,128)S(1)} %bitcast.54), kind=kOutput, calls=%fused_computation.1 | convolution fusion | flops 3626237952 | bytes 18874368 | tf_op jit(solution)/shard_map/dot_general | solution.py:10
  471.5 6.0 %copy.24 = f32[1536,768]{1,0:T(8,128)} copy(f32[1536,768]{0,1:T(8,128)} %fusion) | data formatting | bytes 9437184 | tf_op jit(solution)/shard_map/sub | solution.py:57
  (26 shorter events, 0.6 us)
Async XLA Ops:
  6.5 49.9 %all-gather.7.cloned.1.call-start = ((), (), s32[]{:S(2)}) async-start(), calls=%async_computation.3 | async-start | bytes 3342336 | tf_op jit(solution)/shard_map/all_gather | solution.py:24
  7.3 99.9 %all-gather.5.cloned.1.call-start = ((), (), s32[]{:S(2)}) async-start(), calls=%async_computation.2 | async-start | bytes 1769472 | tf_op jit(solution)/shard_map/all_gather | solution.py:40
  8.6 2.4 collective-permute-start.1
  10.1 0.9 collective-permute-start
  11.7 172.5 %reduce-scatter.5.cloned.1.call-start = ((), (), s32[]{:S(2)}) async-start(), calls=%async_computation.4 | async-start | bytes 1769472 | tf_op jit(solution)/shard_map/reduce_scatter | solution.py:43
  65.0 240.6 %all-reduce.4.cloned.1.call-start = ((), (), s32[]{:S(2)}) async-start(), calls=%async_computation.8 | async-start | bytes 786432 | tf_op jit(solution)/shard_map/psum | solution.py:46
  107.1 77.2 %copy-start = (f32[2,16,16,768]{3,2,1,0:T(8,128)S(1)}, f32[2,16,16,768]{3,2,1,0:T(8,128)}, u32[]{:S(2)}) copy-start(f32[2,16,16,768]{3,2,1,0:T(8,128)} %all-gather.5.cloned.1.call-done) | copy-start | bytes 4718596
  186.7 184.3 %reduce-scatter.7.cloned.1.call-start = ((), (), s32[]{:S(2)}) async-start(), calls=%async_computation.7 | async-start | bytes 3342336
  198.3 1.0 copy-start.2
  198.3 110.5 %copy-start.3 = (f32[64,768]{1,0:T(8,128)S(1)}, f32[64,768]{1,0:T(8,128)}, u32[]{:S(2)}) copy-start(f32[64,768]{1,0:T(8,128)} %reduce-scatter.5.cloned.1.call-done) | copy-start | bytes 589828
  198.3 226.7 %all-gather.9.cloned.1.call-start = ((), (), s32[]{:S(2)}) async-start(), calls=%async_computation.5 | async-start | bytes 1769472 | tf_op jit(solution)/shard_map/all_gather | solution.py:54
  310.1 152.4 %all-gather.11.cloned.1.call-start = ((), (), s32[]{:S(2)}) async-start(), calls=%async_computation.6 | async-start | bytes 3342336 | tf_op jit(solution)/shard_map/all_gather | solution.py:55
  425.0 3.0 copy-start.1
Sparse Core Ops, SparseCore 0:
  9.0 47.4 all-gather.6
  58.8 48.2 all-gather.4
  110.9 73.3 reduce-scatter.4
  186.9 118.7 all-reduce.3
  307.9 63.0 reduce-scatter.6
  373.2 51.7 all-gather.8
  426.7 35.7 all-gather.10
where the time goes:
time: 485 us; the launch traced here: 484 us
  waiting for transfers between devices  403 us (83%)
  matrix products  44.8 us (9%)
  local copies, waits for them, and re-layouts  19.6 us (4%)
  between operations  13.6 us (3%)
    psum x1, waiting for transfers between devices, body(): s_own = lax.psum(mm(p_own, vc, 1, 1), 'col')  106 us
    reduce_scatter x1, waiting for transfers between devices, body(): p_own = lax.psum_scatter(p_part, 'row', scatter_dimension=0, tiled=True)  74.3 us
    unnamed x8, waiting for transfers between devices  61.7 us
    all_gather x1, waiting for transfers between devices, body(): p_all = lax.all_gather(p_own, 'row', axis=0, tiled=True)  45.8 us
    dot_general x12, matrix products, mm(): lax.dot_general(a, b, (((ca,), (cb,)), ((), ())), precision=HIGH, preferr...  44.8 us
    all_gather x1, waiting for transfers between devices, body(): vr = lax.all_gather(vt, 'col', axis=1, tiled=True).reshape(width, rows)  44.7 us
    all_gather x1, waiting for transfers between devices, body(): vc = lax.all_gather(pair, 'row', axis=1, tiled=True).reshape(width, cols)  42.1 us
    all_gather x1, waiting for transfers between devices, body(): z_all = lax.all_gather(z_own, 'col', axis=0, tiled=True)  28.2 us
  transfers between devices with their start and end apart: 9, of which 8 were waited for; matrix products, arithmetic and copies ran while one was open for 10% of the time, Pallas kernels for 0%

commit v1 on v0

--- a/solution.py
+++ b/solution.py
@@ -51,7 +51,9 @@
     )
     p_own = p_own - mm(mm(s_own, tc, 1, 0), vc, 1, 0)
     z_own = mm(y_own, tc, 1, 0)
-    p_all = lax.all_gather(p_own, "row", axis=0, tiled=True)
+    p_all = jnp.concatenate(
+        lax.all_to_all(jnp.stack([p_own] * lax.axis_size("row")), "row", 0, 0), axis=0
+    )
     z_all = lax.all_gather(z_own, "col", axis=0, tiled=True)
     q = mm(tc, p_all, 0, 0)
     return window - mm(vr, q, 0, 0) - mm(z_all, vc, 1, 0)

time: 485 us -> 447 us (0.922)
  waiting for transfers between devices: 403 us -> 359 us
  starting transfers between devices: 2.55 us -> 9.17 us
    all_gather x1 -> x0, waiting for transfers between devices: 45.8 us -> none  [body(): p_all = lax.all_gather(p_own, 'row', axis=0, tiled=True)]
    all_gather x1, waiting for transfers between devices: 28.2 us -> 14 us  [body(): z_all = lax.all_gather(z_own, 'col', axis=0, tiled=True)]
    all_to_all x0 -> x1, waiting for transfers between devices: none -> 13.4 us  [body(): lax.all_to_all(jnp.stack([p_own] * lax.axis_size('row')), 'row', 0, 0)]
    all_to_all x0 -> x1, starting transfers between devices: none -> 6.66 us  [body(): lax.all_to_all(jnp.stack([p_own] * lax.axis_size('row')), 'row', 0, 0)]
    unnamed x8 -> x7, waiting for transfers between devices: 61.7 us -> 64.4 us
    unnamed x14 -> x20, local copies, waits for them, and re-layouts: 10.7 us -> 10.7 us
where the time goes in v1:
time: 447 us
  waiting for transfers between devices  359 us (80%)
  matrix products  42.9 us (10%)
  local copies, waits for them, and re-layouts  20.9 us (5%)
  between operations  13.7 us (3%)
  starting transfers between devices  9.17 us (2%)
    psum x1, waiting for transfers between devices, body(): s_own = lax.psum(mm(p_own, vc, 1, 1), 'col')  106 us
    reduce_scatter x1, waiting for transfers between devices, body(): p_own = lax.psum_scatter(p_part, 'row', scatter_dimension=0, tiled=True)  74.3 us
    unnamed x7, waiting for transfers between devices  64.4 us
    all_gather x1, waiting for transfers between devices, body(): vr = lax.all_gather(vt, 'col', axis=1, tiled=True).reshape(width, rows)  44.7 us
    dot_general x12, matrix products, mm(): lax.dot_general(a, b, (((ca,), (cb,)), ((), ())), precision=HIGH, preferr...  42.9 us
    all_gather x1, waiting for transfers between devices, body(): vc = lax.all_gather(pair, 'row', axis=1, tiled=True).reshape(width, cols)  42.1 us
    all_gather x1, waiting for transfers between devices, body(): z_all = lax.all_gather(z_own, 'col', axis=0, tiled=True)  14 us
    all_to_all x1, waiting for transfers between devices, body(): lax.all_to_all(jnp.stack([p_own] * lax.axis_size('row')), 'row', 0, 0)  13.4 us
  transfers between devices with their start and end apart: 9, of which 8 were waited for; matrix products, arithmetic and copies ran while one was open for 10% of the time, Pallas kernels for 0%

profile of v1, /device:TPU:1, one launch (start us, length us, event | category | flops | bytes accessed | tf_op | source)
XLA Modules:
  0.0 446.6 jit_solution(13340877908266000392)
XLA Ops:
  6.5 0.7 all-gather.6.cloned.1.call-update
  7.3 1.1 reshape.16
  8.6 1.5 collective-permute-start.1
  10.1 0.7 collective-permute-start
  10.7 0.3 collective-permute-done.1
  11.0 0.7 pad_maximum_fusion
  11.8 44.7 %all-gather.6.cloned.1.call-done = f32[2,256,1536]{2,1,0:T(8,128)} async-done(((f32[2,16,1536]{2,1,0:T(8,128)}), f32[2,256,1536]{2,1,0:T(8,128)}) %all-gather.6.cloned.1.call-update) | async-done | bytes 3145744 | tf_op jit(solution)/shard_map/all_gather | solution.py:24
  56.5 8.5 %fusion.21 = f32[512,768]{1,0:T(8,128)} fusion(f32[512,1536]{1,0:T(8,128)} %bitcast.56, f32[1536,768]{1,0:T(8,128)} %param.3), kind=kOutput, calls=%fused_computation.34 | convolution fusion | flops 3623878656 | bytes 9437184 | tf_op jit(solution)/shard_map/dot_general | solution.py:10
  65.1 42.1 %all-gather.4.cloned.1.call-done = f32[2,16,16,768]{3,2,1,0:T(8,128)} async-done(((f32[2,2,16,768]{3,2,1,0:T(8,128)}), f32[2,16,16,768]{3,2,1,0:T(8,128)}) %all-gather.4.cloned.1.call-update) | async-done | bytes 1572880 | tf_op jit(solution)/shard_map/all_gather | solution.py:40
  107.1 1.6 fusion.18
  108.7 1.3 fusion.20
  110.0 74.3 %reduce-scatter.5.cloned.1.call-done = f32[64,768]{1,0:T(8,128)} async-done(((f32[512,768]{1,0:T(8,128)}), f32[64,768]{1,0:T(8,128)}) %reduce-scatter.5.cloned.1.call-update) | async-done | bytes 196624 | tf_op jit(solution)/shard_map/reduce_scatter | solution.py:43
  184.3 2.4 fusion.22
  186.8 7.9 %convolution_bitcast_fusion = f32[1536,512]{0,1:T(8,128)} fusion(f32[512,768]{1,0:T(8,128)S(1)} %bitcast.53, f32[1536,768]{1,0:T(8,128)} %param.3), kind=kOutput, calls=%fused_computation.2 | convolution fusion | flops 3623878656 | bytes 9437184 | tf_op jit(solution)/shard_map/dot_general | solution.py:10
  194.7 3.6 copy.26
  198.6 0.8 copy-done.2
  199.7 106.0 %all-reduce.4.cloned.1.call-done = (f32[64,512]{1,0:T(8,128)}, f32[256,256]{1,0:T(8,128)}) async-done(((f32[64,512]{1,0:T(8,128)}, f32[256,256]{1,0:T(8,128)}), (f32[64,512]{1,0:T(8,128)}, f32[256,256]{1,0:T(8,128)})) %all-reduce.4.cloned.1.call-update) | async-done | bytes 393232 | tf_op jit(solution)/shard_map/psum | solution.py:46
  305.7 1.4 fusion.5
  307.1 0.4 convolution_negate_fusion
  307.5 63.6 %reduce-scatter.7.cloned.1.call-done = f32[96,512]{1,0:T(8,128)} async-done(((f32[1536,512]{1,0:T(8,128)}), f32[96,512]{1,0:T(8,128)}) %reduce-scatter.7.cloned.1.call-update) | async-done | bytes 196624
  371.1 2.1 fusion.1
  373.3 0.5 fusion.3
  373.8 0.6 convolution_subtract_fusion
  374.4 1.3 stack.11
  375.7 6.7 %all-to-all-start = ((f32[8,64,768]{2,1,0:T(8,128)}), f32[8,64,768]{2,1,0:T(8,128)S(1)}, u32[]{:S(2)}, u32[]{:S(2)}) async-start(f32[8,64,768]{2,1,0:T(8,128)} %stack.11), calls=%async_computation.1 | async-start | bytes 3145728 | tf_op jit(solution)/shard_map/all_to_all | solution.py:55
  382.3 6.1 %copy.22 = f32[1536,768]{0,1:T(8,128)} copy(f32[1536,768]{1,0:T(8,128)} %param.3) | data formatting | bytes 9437184 | tf_op args[0]
  388.4 13.4 %all-to-all-done = f32[8,64,768]{2,1,0:T(8,128)S(1)} async-done(((f32[8,64,768]{2,1,0:T(8,128)}), f32[8,64,768]{2,1,0:T(8,128)S(1)}, u32[]{:S(2)}, u32[]{:S(2)}) %all-to-all-start) | async-done | bytes 1572896 | tf_op jit(solution)/shard_map/all_to_all | solution.py:55
  401.8 2.6 fusion.2
  404.4 6.2 %fusion.23 = f32[768,1536]{1,0:T(8,128)} fusion(f32[512,768]{1,0:T(8,128)S(1)} %fusion.2, f32[512,1536]{1,0:T(8,128)S(1)} %bitcast.57), kind=kOutput, calls=%fused_computation.36 | convolution fusion | flops 3623878656 | bytes 9437184 | tf_op jit(solution)/shard_map/dot_general | solution.py:10
  410.7 14.0 %all-gather.8.cloned.1.call-done = f32[1536,512]{1,0:T(8,128)} async-done(((f32[96,512]{1,0:T(8,128)}), f32[1536,512]{1,0:T(8,128)}) %all-gather.8.cloned.1.call-update) | async-done | bytes 3145744 | tf_op jit(solution)/shard_map/all_gather | solution.py:57
  424.7 9.0 %fusion = f32[1536,768]{0,1:T(8,128)} fusion(f32[1536,768]{0,1:T(8,128)} %copy.22, f32[768,1536]{1,0:T(8,128)} %fusion.23, f32[1536,512]{1,0:T(8,128)} %all-gather.8.cloned.1.call-done, f32[512,768]{1,0:T(8,128)S(1)} %bitcast.55), kind=kOutput, calls=%fused_computation.1 | convolution fusion | flops 3626237952 | bytes 18874368 | tf_op jit(solution)/shard_map/dot_general | solution.py:10
  433.7 6.0 %copy.24 = f32[1536,768]{1,0:T(8,128)} copy(f32[1536,768]{0,1:T(8,128)} %fusion) | data formatting | bytes 9437184 | tf_op jit(solution)/shard_map/sub | solution.py:59
  (32 shorter events, 1.0 us)
Async XLA Ops:
  6.5 49.9 %all-gather.6.cloned.1.call-start = ((), (), s32[]{:S(2)}) async-start(), calls=%async_computation.4 | async-start | bytes 3342336 | tf_op jit(solution)/shard_map/all_gather | solution.py:24
  7.3 99.9 %all-gather.4.cloned.1.call-start = ((), (), s32[]{:S(2)}) async-start(), calls=%async_computation.3 | async-start | bytes 1769472 | tf_op jit(solution)/shard_map/all_gather | solution.py:40
  8.6 2.4 collective-permute-start.1
  10.1 0.9 collective-permute-start
  11.7 172.6 %reduce-scatter.5.cloned.1.call-start = ((), (), s32[]{:S(2)}) async-start(), calls=%async_computation.5 | async-start | bytes 1769472 | tf_op jit(solution)/shard_map/reduce_scatter | solution.py:43
  65.0 240.7 %all-reduce.4.cloned.1.call-start = ((), (), s32[]{:S(2)}) async-start(), calls=%async_computation.8 | async-start | bytes 786432 | tf_op jit(solution)/shard_map/psum | solution.py:46
  107.1 77.2 %copy-start = (f32[2,16,16,768]{3,2,1,0:T(8,128)S(1)}, f32[2,16,16,768]{3,2,1,0:T(8,128)}, u32[]{:S(2)}) copy-start(f32[2,16,16,768]{3,2,1,0:T(8,128)} %all-gather.4.cloned.1.call-done) | copy-start | bytes 4718596
  186.8 184.3 %reduce-scatter.7.cloned.1.call-start = ((), (), s32[]{:S(2)}) async-start(), calls=%async_computation.7 | async-start | bytes 3342336
  198.3 1.0 copy-start.2
  198.3 226.4 %all-gather.8.cloned.1.call-start = ((), (), s32[]{:S(2)}) async-start(), calls=%async_computation.6 | async-start | bytes 3342336 | tf_op jit(solution)/shard_map/all_gather | solution.py:57
  199.5 174.3 %copy-start.3 = (f32[1,256,256]{1,2,0:T(8,128)}, f32[1,256,256]{1,2,0:T(8,128)S(1)}, u32[]{:S(2)}) copy-start(f32[1,256,256]{1,2,0:T(8,128)S(1)} %copy.28) | copy-start | bytes 786436
  199.5 174.3 %copy-start.5 = (f32[64,768]{1,0:T(8,128)S(1)}, f32[64,768]{1,0:T(8,128)}, u32[]{:S(2)}) copy-start(f32[64,768]{1,0:T(8,128)} %reduce-scatter.5.cloned.1.call-done) | copy-start | bytes 589828
  199.7 174.7 %copy-start.4 = (f32[1,256,256]{1,2,0:T(8,128)}, f32[1,256,256]{1,2,0:T(8,128)S(1)}, u32[]{:S(2)}) copy-start(f32[1,256,256]{1,2,0:T(8,128)S(1)} %copy.31) | copy-start | bytes 786436
  305.7 67.6 %copy-start.6 = (f32[64,512]{1,0:T(8,128)S(1)}, f32[64,512]{1,0:T(8,128)}, u32[]{:S(2)}) copy-start(f32[64,512]{1,0:T(8,128)} %get-tuple-element.5) | copy-start | bytes 393220
  375.7 26.1 %all-to-all-start = ((f32[8,64,768]{2,1,0:T(8,128)}), f32[8,64,768]{2,1,0:T(8,128)S(1)}, u32[]{:S(2)}, u32[]{:S(2)}) async-start(f32[8,64,768]{2,1,0:T(8,128)} %stack.11), calls=%async_computation.1 | async-start | bytes 3145728 | tf_op jit(solution)/shard_map/all_to_all | solution.py:55
  401.8 2.6 copy-start.1
Sparse Core Ops, SparseCore 0:
  9.0 47.4 all-gather.5
  58.8 48.2 all-gather.3
  110.9 73.3 reduce-scatter.4
  186.9 118.7 all-reduce.3
  307.9 63.0 reduce-scatter.6
  373.4 51.2 all-gather.7
